TPU v7x, 32 devices: a whole 2x2x4 slice. The times are simulated.
32 devices in a mesh: wide: 8 (over y, x, core), narrow: 4 (over z).
Axes of the slice: x: 2, y: 2, z: 4, core: 2. Of those that a mesh axis runs over, the one named last changes fastest.
Arguments:
- short_input: bfloat16 [32, 16, 32, 768], P(('wide', 'narrow')), may hold values from -6 to 6
- long_input: bfloat16 [32, 4, 128, 768], P(('wide', 'narrow')), may hold values from -6 to 6
- short_cotangent: bfloat16 [32, 16, 32, 768], P(('wide', 'narrow')), may hold values from -6 to 6
- long_cotangent: bfloat16 [32, 4, 128, 768], P(('wide', 'narrow')), may hold values from -6 to 6
- short_live: int32 [8], replicated, may hold values from 1 to 16, as said below
- long_live: int32 [8], replicated, may hold values from 1 to 4, as said below
- position_table: bfloat16 [512, 768], replicated, may hold values from -3 to 3
- embed_gain: bfloat16 [768], replicated, may hold values from 0.5 to 1.5
- embed_shift: bfloat16 [768], replicated, may hold values from -1.5 to 1.5
- project_in: bfloat16 [768, 2304], replicated, may hold values from -0.3125 to 0.3125
- query_bias: bfloat16 [768], replicated, may hold values from -1.5 to 1.5
- value_bias: bfloat16 [768], replicated, may hold values from -1.5 to 1.5
- project_out: bfloat16 [768, 768], replicated, may hold values from -0.875 to 0.875
- output_bias: bfloat16 [768], replicated, may hold values from -1.5 to 1.5
- middle_gain: bfloat16 [768], replicated, may hold values from 0.5 to 1.5
- middle_shift: bfloat16 [768], replicated, may hold values from -1.5 to 1.5
- expand_weight: bfloat16 [768, 3072], replicated, may hold values from -0.21875 to 0.21875
- expand_bias: bfloat16 [3072], replicated, may hold values from -1.5 to 1.5
- shrink_weight: bfloat16 [3072, 768], replicated, may hold values from -0.109375 to 0.109375
- shrink_bias: bfloat16 [768], replicated, may hold values from -1.5 to 1.5
- final_gain: bfloat16 [768], replicated, may hold values from 0.5 to 1.5
- final_shift: bfloat16 [768], replicated, may hold values from -1.5 to 1.5
Outputs:
- short_output: bfloat16 [32, 16, 32, 768], P(('wide', 'narrow'))
- long_output: bfloat16 [32, 4, 128, 768], P(('wide', 'narrow'))
- short_input_grad: bfloat16 [32, 16, 32, 768], P(('wide', 'narrow'))
- long_input_grad: bfloat16 [32, 4, 128, 768], P(('wide', 'narrow'))
- position_grad: float32 [512, 768], P(None, ('wide', 'narrow'))
- embed_gain_grad: float32 [768], P(('wide', 'narrow'))
- embed_shift_grad: float32 [768], P(('wide', 'narrow'))
- project_in_grad: float32 [768, 2304], P(('wide', 'narrow'))
- query_bias_grad: float32 [768], P(('wide', 'narrow'))
- value_bias_grad: float32 [768], P(('wide', 'narrow'))
- project_out_grad: float32 [768, 768], P(('wide', 'narrow'))
- output_bias_grad: float32 [768], P(('wide', 'narrow'))
- middle_gain_grad: float32 [768], P(('wide', 'narrow'))
- middle_shift_grad: float32 [768], P(('wide', 'narrow'))
- expand_weight_grad: float32 [768, 3072], P(('wide', 'narrow'))
- expand_bias_grad: float32 [3072], P(('wide', 'narrow'))
- shrink_weight_grad: float32 [3072, 768], P(('wide', 'narrow'))
- shrink_bias_grad: float32 [768], P(('wide', 'narrow'))
- final_gain_grad: float32 [768], P(('wide', 'narrow'))
- final_shift_grad: float32 [768], P(('wide', 'narrow'))
Inputs may be any that keep to these rules, and one draw needn't show every extreme that they name: `short_live`: entry (w // 4) * 4 + n counts the live short rows, rows 0 to that count - 1, of the group of wide index w and narrow index n; some group has all 16 live. `long_live`: likewise for the long rows; some group has all 4 live.
All inputs are finite; a program needn't handle non-finite values.
Results may differ from a plain program's by a relative error of at most 0.015.
Values may be sent and summed in bfloat16 or wider, within the bound.
No kernel may reach another device: no remote copies, remote signals or barrier semaphores. Data moves between devices by JAX's collectives and lax.ppermute only.
A program may use at most 256 MiB of HBM per device.

v0:
```python
import jax
import jax.numpy as jnp
from jax import lax
from jax.sharding import PartitionSpec as P

D = 768
HEADS = 12
HEAD_DIM = 64


EPS = 1e-05


def partner(shard, axis, apart):
    return lax.ppermute(shard, axis, [(i, i ^ 1 << apart) for i in range(lax.axis_size(axis))])


def norm_rows(values, row_gain, row_shift):
    row_mean = jnp.mean(values, axis=-1, keepdims=True)
    centered = values - row_mean
    spread = jnp.mean(centered * centered, axis=-1, keepdims=True)
    return centered * lax.rsqrt(spread + EPS) * row_gain + row_shift


def exact_gelu(values):
    return jax.nn.gelu(values, approximate=False)


def left_product(left_side, right_side):
    return lax.dot_general(
        left_side, right_side, (((0,), (0,)), ((), ())), preferred_element_type=jnp.float32
    )


def right_product(grad_rows, weight):
    return lax.dot_general(
        grad_rows, weight, (((1,), (1,)), ((), ())), preferred_element_type=jnp.float32
    )


def select_half(tensor, bit_value, axis_pos):
    return lax.dynamic_index_in_dim(tensor, bit_value, axis_pos, keepdims=False)


def order_pair(own_part, their_part, bit_value, axis_pos):
    return lax.cond(
        bit_value == 0,
        lambda: jnp.stack([own_part, their_part], axis_pos),
        lambda: jnp.stack([their_part, own_part], axis_pos),
    )


def quad_exchange(tensor):
    wide_index = lax.axis_index("wide")
    low_bit = wide_index % 2
    high_bit = wide_index // 2 % 2
    shaped = tensor.reshape((2, 2) + tensor.shape[1:])
    staying = select_half(shaped, low_bit, 1)
    outgoing = select_half(shaped, 1 - low_bit, 1)
    incoming = partner(outgoing, "wide", 0)
    mixed = order_pair(staying, incoming, low_bit, 1)
    staying = select_half(mixed, high_bit, 0)
    outgoing = select_half(mixed, 1 - high_bit, 0)
    incoming = partner(outgoing, "wide", 1)
    return order_pair(staying, incoming, high_bit, 0).reshape(tensor.shape)


def attend(heads):
    query_rows = heads[:, :, :, 0]
    key_rows = heads[:, :, :, 1]
    value_rows = heads[:, :, :, 2]
    factor = query_rows.shape[-1] ** (-0.5)
    scores = (
        jnp.einsum("crthd,Crshd->rhctCs", query_rows, key_rows, preferred_element_type=jnp.float32)
        * factor
    )
    highest = jnp.max(scores, axis=(4, 5), keepdims=True)
    totals = jnp.sum(jnp.exp(scores - highest), axis=(4, 5), keepdims=True)
    log_total = highest + jnp.log(totals)
    weights = jnp.exp(scores - log_total).astype(jnp.bfloat16)
    context = jnp.einsum(
        "rhctCs,Crshd->crthd", weights, value_rows, preferred_element_type=jnp.float32
    )
    return (context.astype(jnp.bfloat16), log_total)


def attend_back(heads, log_total, context_grad):
    query_rows = heads[:, :, :, 0]
    key_rows = heads[:, :, :, 1]
    value_rows = heads[:, :, :, 2]
    factor = query_rows.shape[-1] ** (-0.5)
    scores = (
        jnp.einsum("crthd,Crshd->rhctCs", query_rows, key_rows, preferred_element_type=jnp.float32)
        * factor
    )
    soft_weights = jnp.exp(scores - log_total)
    value_grad = jnp.einsum(
        "rhctCs,crthd->Crshd",
        soft_weights.astype(jnp.bfloat16),
        context_grad,
        preferred_element_type=jnp.float32,
    )
    prob_grad = jnp.einsum(
        "crthd,Crshd->rhctCs", context_grad, value_rows, preferred_element_type=jnp.float32
    )
    row_inner = jnp.sum(soft_weights * prob_grad, axis=(4, 5), keepdims=True)
    score_grad = (soft_weights * (prob_grad - row_inner) * factor).astype(jnp.bfloat16)
    query_grad = jnp.einsum(
        "rhctCs,Crshd->crthd", score_grad, key_rows, preferred_element_type=jnp.float32
    )
    key_grad = jnp.einsum(
        "rhctCs,crthd->Crshd", score_grad, query_rows, preferred_element_type=jnp.float32
    )
    return jnp.stack([query_grad, key_grad, value_grad], axis=3).astype(jnp.bfloat16)


def on_device(
    short_input,
    long_input,
    short_cotangent,
    long_cotangent,
    short_live,
    long_live,
    position_table,
    embed_gain,
    embed_shift,
    project_in,
    query_bias,
    value_bias,
    project_out,
    output_bias,
    middle_gain,
    middle_shift,
    expand_weight,
    expand_bias,
    shrink_weight,
    shrink_bias,
    final_gain,
    final_shift,
):
    float_type = jnp.float32
    part_heads = HEADS // 4
    part_width = D // 4
    wide_index = lax.axis_index("wide")
    span_index = wide_index % 4
    group_index = wide_index // 4 * lax.axis_size("narrow") + lax.axis_index("narrow")
    short_count = lax.dynamic_index_in_dim(short_live, group_index, 0, keepdims=False)
    long_count = lax.dynamic_index_in_dim(long_live, group_index, 0, keepdims=False)
    short_span = short_input.shape[2]
    long_span = long_input.shape[2]
    pos_table = position_table.astype(float_type)
    short_start = span_index * short_span
    long_start = span_index * long_span
    short_pos = lax.dynamic_slice_in_dim(pos_table, short_start, short_span, 0).reshape(
        1, 1, short_span, D
    )
    long_pos = lax.dynamic_slice_in_dim(pos_table, long_start, long_span, 0).reshape(
        1, 1, long_span, D
    )
    blocks = short_input.shape[0]
    short_rows = short_input.shape[1]
    long_rows = long_input.shape[1]
    short_size = blocks * short_rows * short_span
    short_mask = (jnp.arange(short_rows) < short_count).astype(float_type)
    long_mask = (jnp.arange(long_rows) < long_count).astype(float_type)
    token_mask = jnp.concatenate(
        [
            jnp.broadcast_to(short_mask[None, :, None], (blocks, short_rows, short_span)).reshape(
                -1
            ),
            jnp.broadcast_to(long_mask[None, :, None], (blocks, long_rows, long_span)).reshape(-1),
        ]
    )[:, None]
    embedded = jnp.concatenate(
        [
            (short_input.astype(float_type) + short_pos).reshape(-1, D),
            (long_input.astype(float_type) + long_pos).reshape(-1, D),
        ]
    )
    cotangent = (
        jnp.concatenate([short_cotangent.reshape(-1, D), long_cotangent.reshape(-1, D)]).astype(
            float_type
        )
        * token_mask
    )
    base, embed_back = jax.vjp(
        norm_rows, embedded, embed_gain.astype(float_type), embed_shift.astype(float_type)
    )
    base_low = base.astype(jnp.bfloat16)
    bias_all = jnp.concatenate([query_bias, jnp.zeros_like(query_bias), value_bias]).astype(
        float_type
    )
    short_base = base_low[:short_size]
    long_base = base_low[short_size:]
    weight_parts = (
        project_in.reshape(D, 3, 4, part_width).transpose(2, 0, 1, 3).reshape(4, D, 3 * part_width)
    )
    bias_parts = bias_all.reshape(3, 4, part_width).transpose(1, 0, 2).reshape(4, 1, 3 * part_width)
    out_parts = project_out.reshape(4, part_width, D)
    short_triple = (
        jnp.einsum("td,qdf->qtf", short_base, weight_parts, preferred_element_type=float_type)
        + bias_parts
    ).astype(jnp.bfloat16)
    long_triple = (
        jnp.einsum("td,qdf->qtf", long_base, weight_parts, preferred_element_type=float_type)
        + bias_parts
    ).astype(jnp.bfloat16)
    short_heads = quad_exchange(short_triple).reshape(
        4, short_rows, short_span, 3, part_heads, HEAD_DIM
    )
    long_heads = quad_exchange(long_triple).reshape(
        4, long_rows, long_span, 3, part_heads, HEAD_DIM
    )
    short_context, short_total = attend(short_heads)
    long_context, long_total = attend(long_heads)
    short_ctx = quad_exchange(short_context.reshape(4, -1, part_width))
    long_ctx = quad_exchange(long_context.reshape(4, -1, part_width))
    branch = jnp.concatenate(
        [
            jnp.einsum("qtf,qfe->te", short_ctx, out_parts, preferred_element_type=float_type),
            jnp.einsum("qtf,qfe->te", long_ctx, out_parts, preferred_element_type=float_type),
        ]
    )
    branch = branch + output_bias.astype(float_type)
    middle, middle_back = jax.vjp(
        norm_rows, base + branch, middle_gain.astype(float_type), middle_shift.astype(float_type)
    )
    middle_low = middle.astype(jnp.bfloat16)
    expanded = jnp.dot(
        middle_low, expand_weight, preferred_element_type=float_type
    ) + expand_bias.astype(float_type)
    activated, gelu_back = jax.vjp(exact_gelu, expanded)
    activated_low = activated.astype(jnp.bfloat16)
    shrunk = jnp.dot(
        activated_low, shrink_weight, preferred_element_type=float_type
    ) + shrink_bias.astype(float_type)
    result, final_back = jax.vjp(
        norm_rows, middle + shrunk, final_gain.astype(float_type), final_shift.astype(float_type)
    )
    output = (result * token_mask).astype(jnp.bfloat16)
    final_grad, final_gain_grad, final_shift_grad = final_back(cotangent)
    shrunk_grad = final_grad.astype(jnp.bfloat16)
    shrink_weight_grad = left_product(activated_low, shrunk_grad)
    shrink_bias_grad = jnp.sum(shrunk_grad.astype(float_type), axis=0)
    (expanded_grad,) = gelu_back(right_product(shrunk_grad, shrink_weight))
    expanded_low = expanded_grad.astype(jnp.bfloat16)
    expand_weight_grad = left_product(middle_low, expanded_low)
    expand_bias_grad = jnp.sum(expanded_low.astype(float_type), axis=0)
    middle_grad = final_grad + right_product(expanded_low, expand_weight)
    mixed_grad, middle_gain_grad, middle_shift_grad = middle_back(middle_grad)
    branch_grad = mixed_grad.astype(jnp.bfloat16)
    output_bias_grad = jnp.sum(branch_grad.astype(float_type), axis=0)
    short_bgrad = branch_grad[:short_size]
    long_bgrad = branch_grad[short_size:]
    project_out_grad = (
        jnp.einsum("qtf,te->qfe", short_ctx, short_bgrad, preferred_element_type=float_type)
        + jnp.einsum("qtf,te->qfe", long_ctx, long_bgrad, preferred_element_type=float_type)
    ).reshape(D, D)
    short_cgrad = jnp.einsum(
        "te,qfe->qtf", short_bgrad, out_parts, preferred_element_type=float_type
    ).astype(jnp.bfloat16)
    long_cgrad = jnp.einsum(
        "te,qfe->qtf", long_bgrad, out_parts, preferred_element_type=float_type
    ).astype(jnp.bfloat16)
    short_back = quad_exchange(short_cgrad).reshape(4, short_rows, short_span, part_heads, HEAD_DIM)
    long_back = quad_exchange(long_cgrad).reshape(4, long_rows, long_span, part_heads, HEAD_DIM)
    short_tgrad = attend_back(short_heads, short_total, short_back)
    long_tgrad = attend_back(long_heads, long_total, long_back)
    short_arrived = quad_exchange(short_tgrad.reshape(4, -1, 3 * part_width))
    long_arrived = quad_exchange(long_tgrad.reshape(4, -1, 3 * part_width))
    grad_parts = jnp.einsum(
        "td,qtf->qdf", short_base, short_arrived, preferred_element_type=float_type
    ) + jnp.einsum("td,qtf->qdf", long_base, long_arrived, preferred_element_type=float_type)
    project_in_grad = (
        grad_parts.reshape(4, D, 3, part_width).transpose(1, 2, 0, 3).reshape(D, 3 * D)
    )
    column_sums = (
        jnp.sum(short_arrived.astype(float_type), axis=1)
        + jnp.sum(long_arrived.astype(float_type), axis=1)
    ).reshape(4, 3, part_width)
    query_bias_grad = column_sums[:, 0].reshape(D)
    value_bias_grad = column_sums[:, 2].reshape(D)
    base_grad = mixed_grad + jnp.concatenate(
        [
            jnp.einsum(
                "qtf,qdf->td", short_arrived, weight_parts, preferred_element_type=float_type
            ),
            jnp.einsum(
                "qtf,qdf->td", long_arrived, weight_parts, preferred_element_type=float_type
            ),
        ]
    )
    embed_grad, embed_gain_grad, embed_shift_grad = embed_back(base_grad)
    input_grad = embed_grad.astype(jnp.bfloat16)
    short_sum = jnp.sum(
        embed_grad[:short_size].reshape(blocks, short_rows, short_span, D), axis=1
    ).reshape(-1, D)
    long_sum = jnp.sum(
        embed_grad[short_size:].reshape(blocks, long_rows, long_span, D), axis=1
    ).reshape(-1, D)
    empty_table = jnp.zeros(pos_table.shape, float_type)
    position_grad = lax.dynamic_update_slice_in_dim(
        empty_table, short_sum, short_start, 0
    ) + lax.dynamic_update_slice_in_dim(empty_table, long_sum, long_start, 0)
    short_out = output[:short_size].reshape(blocks, short_rows, short_span, D)
    long_out = output[short_size:].reshape(blocks, long_rows, long_span, D)
    short_dgrad = input_grad[:short_size].reshape(blocks, short_rows, short_span, D)
    long_dgrad = input_grad[short_size:].reshape(blocks, long_rows, long_span, D)
    summed = (
        lax.psum_scatter(position_grad, ("wide", "narrow"), scatter_dimension=1, tiled=True),
        lax.psum_scatter(embed_gain_grad, ("wide", "narrow"), scatter_dimension=0, tiled=True),
        lax.psum_scatter(embed_shift_grad, ("wide", "narrow"), scatter_dimension=0, tiled=True),
        lax.psum_scatter(project_in_grad, ("wide", "narrow"), scatter_dimension=0, tiled=True),
        lax.psum_scatter(query_bias_grad, ("wide", "narrow"), scatter_dimension=0, tiled=True),
        lax.psum_scatter(value_bias_grad, ("wide", "narrow"), scatter_dimension=0, tiled=True),
        lax.psum_scatter(project_out_grad, ("wide", "narrow"), scatter_dimension=0, tiled=True),
        lax.psum_scatter(output_bias_grad, ("wide", "narrow"), scatter_dimension=0, tiled=True),
        lax.psum_scatter(middle_gain_grad, ("wide", "narrow"), scatter_dimension=0, tiled=True),
        lax.psum_scatter(middle_shift_grad, ("wide", "narrow"), scatter_dimension=0, tiled=True),
        lax.psum_scatter(expand_weight_grad, ("wide", "narrow"), scatter_dimension=0, tiled=True),
        lax.psum_scatter(expand_bias_grad, ("wide", "narrow"), scatter_dimension=0, tiled=True),
        lax.psum_scatter(shrink_weight_grad, ("wide", "narrow"), scatter_dimension=0, tiled=True),
        lax.psum_scatter(shrink_bias_grad, ("wide", "narrow"), scatter_dimension=0, tiled=True),
        lax.psum_scatter(final_gain_grad, ("wide", "narrow"), scatter_dimension=0, tiled=True),
        lax.psum_scatter(final_shift_grad, ("wide", "narrow"), scatter_dimension=0, tiled=True),
    )
    return (
        short_out,
        long_out,
        short_dgrad,
        long_dgrad,
        summed[0],
        summed[1],
        summed[2],
        summed[3],
        summed[4],
        summed[5],
        summed[6],
        summed[7],
        summed[8],
        summed[9],
        summed[10],
        summed[11],
        summed[12],
        summed[13],
        summed[14],
        summed[15],
    )


def solution(mesh):
    in_specs = (
        P(("wide", "narrow"), None, None, None),
        P(("wide", "narrow"), None, None, None),
        P(("wide", "narrow"), None, None, None),
        P(("wide", "narrow"), None, None, None),
        P(),
        P(),
        P(),
        P(),
        P(),
        P(),
        P(),
        P(),
        P(),
        P(),
        P(),
        P(),
        P(),
        P(),
        P(),
        P(),
        P(),
        P(),
    )
    out_specs = (
        P(("wide", "narrow"), None, None, None),
        P(("wide", "narrow"), None, None, None),
        P(("wide", "narrow"), None, None, None),
        P(("wide", "narrow"), None, None, None),
        P(None, ("wide", "narrow")),
        P(("wide", "narrow")),
        P(("wide", "narrow")),
        P(("wide", "narrow"), None),
        P(("wide", "narrow")),
        P(("wide", "narrow")),
        P(("wide", "narrow"), None),
        P(("wide", "narrow")),
        P(("wide", "narrow")),
        P(("wide", "narrow")),
        P(("wide", "narrow"), None),
        P(("wide", "narrow")),
        P(("wide", "narrow"), None),
        P(("wide", "narrow")),
        P(("wide", "narrow")),
        P(("wide", "narrow")),
    )
    return jax.shard_map(
        on_device, mesh=mesh, in_specs=in_specs, out_specs=out_specs, check_vma=False
    )
```

profile of v0, /device:TPU:0, one launch (start us, length us, event | category | flops | bytes accessed | tf_op | source)
XLA Modules:
  0.0 1069.3 jit_solution(13391769561974852060)
XLA Ops:
  67.0 9.7 collective-permute-done.5
  76.8 8.8 conditional.21
  94.6 9.6 fusion.7
  112.0 26.6 %conditional.17 = (bf16[4,16,32,3,3,64]{5,4,3,2,1,0:T(4,128)(2,1)}) conditional(s32[]{:T(128)} %convert_element_type.193, (bf16[2,512,576]{1,2,0:T(8,128)(2,1)}, bf16[2,512,576]{2,1,0:T(8,128)(2,1)}) %tuple.182, (bf16[2,512,576]{2,1,0:T(8,128)(2,1)}, bf16[2,512,576]{1,2,0:T(8,128)(2,1)}) %tuple.183), branch_computations={%region_4.5_spmd, %region_5.6_spmd} | conditional | flops 1179648 | bytes 11796488 | solution.py:46
  118.1 12.1 %reshape_reshape.43 = bf16[4,16,32,3,3,64]{5,4,3,2,1,0:T(4,128)(2,1)} reshape(bf16[2,2,512,576]{3,2,1,0:T(8,128)(2,1)} %pad_maximum_fusion.3) | data formatting | bytes 4718592 | tf_op jit(solution)/shard_map/reshape;reshape | solution.py:208
  184.6 7.8 collective-permute-done.7
  210.4 35.0 %multiply_convert_fusion.2 = (bf16[1024,3072]{1,0:T(8,128)(2,1)S(1)}, f32[1024,3072]{1,0:T(8,128)}, f32[1024,3072]{1,0:T(8,128)}) fusion(f32[3072]{0:T(1024)S(1)} %convert_element_type.210, bf16[768,3072]{1,0:T(8,128)(2,1)S(1)} %bitcast.524, f32[1024,768]{1,0:T(8,128)S(1)} %get-tuple-element.627, f32[768]{0:T(1024)S(1)} %convert_element_type.208, ...), kind=kOutput, calls=%fused_computation.44 | convolution fusion | flops 5043388416 | bytes 39348224 | tf_op jit(solution)/shard_map/dot_general | solution.py:229
  261.6 17.9 %convert_reduce_fusion.4 = (f32[3072]{0:T(1024)}, bf16[1024,3072]{1,0:T(8,128)(2,1)}) fusion(f32[1024,3072]{1,0:T(8,128)} %get-tuple-element.625, bf16[1024,768]{1,0:T(8,128)(2,1)S(1)} %get-tuple-element.614, bf16[3072,768]{1,0:T(8,128)(2,1)} %param.72, f32[1024,3072]{1,0:T(8,128)} %get-tuple-element.677, f32[3072]{0:T(1024)S(1)} %convert_element_type.210), kind=kOutput, calls=%fused_computation.38 | convolution fusion | flops 4885312512 | bytes 37773312 | tf_op jit(solution)/shard_map/dot_general | solution.py:36
  279.5 10.6 multiply_reduce_fusion.5
  323.2 10.3 multiply_reduce_fusion
  352.0 9.1 fusion.24
  361.1 10.8 %multiply_reduce_fusion.1 = (f32[16,3,4,32]{3,2,1,0:T(4,128)}, f32[16,3,4,32,4,32]{3,5,4,2,1,0:T(8,128)}) fusion(f32[16,3,4,32,4,32]{3,5,4,2,1,0:T(8,128)} %copy-done.2, f32[16,3,4,32]{3,2,1,0:T(4,128)S(1)} %copy-done.48, bf16[4,16,32,1,3,64]{5,4,3,2,1,0:T(4,128)(2,1)S(1)} %copy-done.17, bf16[4,16,32,3,64,1]{4,3,2,1,0,5:T(4,128)(2,1)S(1)} %bitcast.451), kind=kOutput, calls=%fused_computation.42 | convolution fusion | flops 103802880 | bytes 7913472 | tf_op jit(solution)/shard_map/crthd,Crshd->rhctCs/dot_general | solution.py:103
  379.7 10.2 multiply_convert_fusion.1
  401.7 11.6 %convert_element_type.225 = bf16[2,2,512,576]{3,2,1,0:T(8,128)(2,1)} reshape(bf16[4,16,32,3,3,64]{5,4,3,2,1,0:T(4,128)(2,1)} %copy.355) | data formatting | bytes 4718592 | tf_op jit(solution)/shard_map/convert_element_type | solution.py:114
  450.1 9.7 collective-permute-done.15
  472.5 12.6 %collective-permute-done.11 = bf16[2,512,576]{1,2,0:T(8,128)(2,1)} collective-permute-done((bf16[2,512,576]{1,2,0:T(8,128)(2,1)}, bf16[2,512,576]{1,2,0:T(8,128)(2,1)}, u32[]{:S(2)}, u32[]{:S(2)}) %collective-permute-start.11) | collective-permute-done | bytes 1179680 | tf_op jit(solution)/shard_map/ppermute | solution.py:15
  518.4 8.0 copy.434
  527.1 11.0 %fusion.51 = f32[768,3072]{1,0:T(8,128)} fusion(bf16[1024,3072]{1,0:T(8,128)(2,1)} %get-tuple-element.686, f32[1024,768]{1,0:T(8,128)} %copy-done.8, f32[768]{0:T(1024)S(1)} %copy-done.69, f32[768]{0:T(1024)S(1)} %copy-done.67, f32[1024]{0:T(1024)S(1)} %copy-done.59, f32[1024]{0:T(1024)S(1)} %copy-done.57), kind=kOutput, calls=%fused_computation.215 | convolution fusion | flops 4835770368 | bytes 18888704 | tf_op jit(solution)/shard_map/dot_general | solution.py:30
  539.6 10.2 fusion.68
  552.7 41.9 %all-reduce.11 = (f32[768]{0:T(1024)S(1)}, f32[768]{0:T(1024)S(1)}, f32[768]{0:T(1024)S(1)}, f32[768]{0:T(1024)S(1)}, f32[768]{0:T(1024)S(1)}, /*index=5*/f32[76...) all-reduce(f32[768]{0:T(1024)S(1)} %get-tuple-element.590, ...), channel_id=3, replica_groups=mesh['wide'=8,'narrow'=4] {'wide','narrow'}, use_global_device_ids=true, to_apply=%region_58.59.clone | all-reduce | flops 10752 | bytes 86016
  603.7 50.6 %reduce-scatter.16.cloned.1.call-done = f32[24,512]{1,0:T(8,128)} async-done(((f32[768,512]{1,0:T(8,128)}), f32[24,512]{1,0:T(8,128)}) %reduce-scatter.16.cloned.1.call-update) | async-done | bytes 49168
  654.2 125.2 %reduce-scatter.18.cloned.1.call-done = f32[24,2304]{1,0:T(8,128)} async-done(((f32[768,2304]{1,0:T(8,128)}), f32[24,2304]{1,0:T(8,128)}) %reduce-scatter.18.cloned.1.call-update) | async-done | bytes 221200
  779.5 141.2 %reduce-scatter.12.cloned.1.call-done = f32[24,3072]{1,0:T(8,128)} async-done(((f32[768,3072]{1,0:T(8,128)}), f32[24,3072]{1,0:T(8,128)}) %reduce-scatter.12.cloned.1.call-update) | async-done | bytes 294928 | tf_op jit(solution)/shard_map/reduce_scatter | solution.py:320
  920.7 141.7 %reduce-scatter.14.cloned.1.call-done = f32[96,768]{1,0:T(8,128)} async-done(((f32[3072,768]{1,0:T(8,128)}), f32[96,768]{1,0:T(8,128)}) %reduce-scatter.14.cloned.1.call-update) | async-done | bytes 294928 | tf_op jit(solution)/shard_map/reduce_scatter | solution.py:322
  (425 shorter events, 399.6 us)
Async XLA Ops:
  7.2 187.6 %copy-start = (bf16[768,768]{1,0:T(8,128)(2,1)S(1)}, bf16[768,768]{1,0:T(8,128)(2,1)}, u32[]{:S(2)}) copy-start(bf16[768,768]{1,0:T(8,128)(2,1)} %param.66) | copy-start | bytes 3538948
  7.2 596.5 %reduce-scatter.10.cloned.1.call-start = ((), (), s32[]{:S(2)}) async-start(), calls=%async_computation.5 | async-start | bytes 2433024 | tf_op jit(solution)/shard_map/reduce_scatter | solution.py:316
  19.1 188.4 %copy-start.62 = (f32[768]{0:T(1024)}, f32[768]{0:T(1024)S(1)}, u32[]{:S(2)}) copy-start(f32[768]{0:T(1024)S(1)} %convert_element_type.191) | copy-start | bytes 9220
  20.6 186.9 %copy-start.3 = (f32[1,4,128,768]{3,2,1,0:T(8,128)}, f32[1,4,128,768]{3,2,1,0:T(8,128)S(1)}, u32[]{:S(2)}) copy-start(f32[1,4,128,768]{3,2,1,0:T(8,128)S(1)} %convert_add_fusion) | copy-start | bytes 4718596
  28.3 6.7 collective-permute-start.4
  32.4 22.8 %collective-permute-start = (bf16[2,512,576]{1,2,0:T(8,128)(2,1)}, bf16[2,512,576]{1,2,0:T(8,128)(2,1)}, u32[]{:S(2)}, u32[]{:S(2)}) collective-permute-start(bf16[2,512,576]{1,2,0:T(8,128)(2,1)} %get-tuple-element.647), channel_id=1, source_target_pairs={{0,4},{4,0},{8,12},{12,8},{16,20},{20,16},{24,28},{28,24},{1,5},{5... | collective-permute-start | bytes 3538952 | tf_op jit(solution)/shard_map/ppermute | solution.py:15
  46.8 30.0 %collective-permute-start.5 = (bf16[2,512,576]{1,2,0:T(8,128)(2,1)}, bf16[2,512,576]{1,2,0:T(8,128)(2,1)}, u32[]{:S(2)}, u32[]{:S(2)}) collective-permute-start(bf16[2,512,576]{1,2,0:T(8,128)(2,1)} %bitcast.509), channel_id=1, source_target_pairs={{0,8},{4,12},{8,0},{12,4},{16,24},{20,28},{24,16},{28,20},{1,9},{5... | collective-permute-start | bytes 3538952 | tf_op jit(solution)/shard_map/ppermute | solution.py:15
  67.0 45.0 %collective-permute-start.1 = (bf16[2,512,576]{1,2,0:T(8,128)(2,1)}, bf16[2,512,576]{1,2,0:T(8,128)(2,1)}, u32[]{:S(2)}, u32[]{:S(2)}) collective-permute-start(bf16[2,512,576]{1,2,0:T(8,128)(2,1)} %bitcast.511), channel_id=1, source_target_pairs={{0,8},{4,12},{8,0},{12,4},{16,24},{20,28},{24,16},{28,20},{1,9},{5... | collective-permute-start | bytes 3538952 | tf_op jit(solution)/shard_map/ppermute | solution.py:15
  112.0 56.3 %collective-permute-start.6 = (bf16[2,512,192]{1,2,0:T(8,128)(2,1)}, bf16[2,512,192]{1,2,0:T(8,128)(2,1)}, u32[]{:S(2)}, u32[]{:S(2)}) collective-permute-start(bf16[2,512,192]{1,2,0:T(8,128)(2,1)} %get-tuple-element.672), channel_id=1, source_target_pairs={{0,4},{4,0},{8,12},{12,8},{16,20},{20,16},{24,28},{28,24},{1,5},{5... | collective-permute-start | bytes 1179656 | tf_op jit(solution)/shard_map/ppermute | solution.py:15
  166.4 13.0 %collective-permute-start.2 = (bf16[2,512,192]{2,1,0:T(8,128)(2,1)}, bf16[2,512,192]{2,1,0:T(8,128)(2,1)}, u32[]{:S(2)}, u32[]{:S(2)}) collective-permute-start(bf16[2,512,192]{2,1,0:T(8,128)(2,1)} %get-tuple-element.664), channel_id=1, source_target_pairs={{0,4},{4,0},{8,12},{12,8},{16,20},{20,16},{24,28},{28,24},{1,5},{5... | collective-permute-start | bytes 1179656 | tf_op jit(solution)/shard_map/ppermute | solution.py:15
  177.3 15.1 %collective-permute-start.7 = (bf16[2,512,192]{2,1,0:T(8,128)(2,1)}, bf16[2,512,192]{2,1,0:T(8,128)(2,1)}, u32[]{:S(2)}, u32[]{:S(2)}) collective-permute-start(bf16[2,512,192]{2,1,0:T(8,128)(2,1)} %get-tuple-element.666), channel_id=1, source_target_pairs={{0,8},{4,12},{8,0},{12,4},{16,24},{20,28},{24,16},{28,20},{1,9},{5... | collective-permute-start | bytes 1179656 | tf_op jit(solution)/shard_map/ppermute | solution.py:15
  183.7 19.3 %collective-permute-start.3 = (bf16[2,512,192]{2,1,0:T(8,128)(2,1)}, bf16[2,512,192]{2,1,0:T(8,128)(2,1)}, u32[]{:S(2)}, u32[]{:S(2)}) collective-permute-start(bf16[2,512,192]{2,1,0:T(8,128)(2,1)} %get-tuple-element.662), channel_id=1, source_target_pairs={{0,8},{4,12},{8,0},{12,4},{16,24},{20,28},{24,16},{28,20},{1,9},{5... | collective-permute-start | bytes 1179656 | tf_op jit(solution)/shard_map/ppermute | solution.py:15
  295.6 4.4 collective-permute-start.12
  299.5 5.9 collective-permute-start.8
  302.3 12.2 %collective-permute-start.13 = (bf16[2,512,192]{1,2,0:T(8,128)(2,1)}, bf16[2,512,192]{1,2,0:T(8,128)(2,1)S(1)}, u32[]{:S(2)}, u32[]{:S(2)}) collective-permute-start(bf16[2,512,192]{1,2,0:T(8,128)(2,1)} %bitcast.174), channel_id=1, source_target_pairs={{0,8},{4,12},{8,0},{12,4},{16,24},{20,28},{24,16},{28,20},{1,9},{5... | collective-permute-start | bytes 1179656 | tf_op jit(solution)/shard_map/ppermute | solution.py:15
  307.6 38.2 %collective-permute-start.9 = (bf16[2,512,192]{2,1,0:T(8,128)(2,1)}, bf16[2,512,192]{2,1,0:T(8,128)(2,1)}, u32[]{:S(2)}, u32[]{:S(2)}) collective-permute-start(bf16[2,512,192]{2,1,0:T(8,128)(2,1)} %get-tuple-element.658), channel_id=1, source_target_pairs={{0,8},{4,12},{8,0},{12,4},{16,24},{20,28},{24,16},{28,20},{1,9},{5... | collective-permute-start | bytes 1179656 | tf_op jit(solution)/shard_map/ppermute | solution.py:15
  379.7 39.8 %collective-permute-start.14 = (bf16[2,512,576]{1,2,0:T(8,128)(2,1)}, bf16[2,512,576]{1,2,0:T(8,128)(2,1)S(1)}, u32[]{:S(2)}, u32[]{:S(2)}) collective-permute-start(bf16[2,512,576]{1,2,0:T(8,128)(2,1)} %get-tuple-element.645), channel_id=1, source_target_pairs={{0,4},{4,0},{8,12},{12,8},{16,20},{20,16},{24,28},{28,24},{1,5},{5... | collective-permute-start | bytes 3538952 | tf_op jit(solution)/shard_map/ppermute | solution.py:15
  419.1 14.2 %collective-permute-start.10 = (bf16[2,512,576]{1,2,0:T(8,128)(2,1)}, bf16[2,512,576]{1,2,0:T(8,128)(2,1)}, u32[]{:S(2)}, u32[]{:S(2)}) collective-permute-start(bf16[2,512,576]{1,2,0:T(8,128)(2,1)} %bitcast.513), channel_id=1, source_target_pairs={{0,4},{4,0},{8,12},{12,8},{16,20},{20,16},{24,28},{28,24},{1,5},{5... | collective-permute-start | bytes 3538952 | tf_op jit(solution)/shard_map/ppermute | solution.py:15
  431.4 28.4 %collective-permute-start.15 = (bf16[2,512,576]{1,2,0:T(8,128)(2,1)}, bf16[2,512,576]{1,2,0:T(8,128)(2,1)}, u32[]{:S(2)}, u32[]{:S(2)}) collective-permute-start(bf16[2,512,576]{1,2,0:T(8,128)(2,1)} %bitcast.510), channel_id=1, source_target_pairs={{0,8},{4,12},{8,0},{12,4},{16,24},{20,28},{24,16},{28,20},{1,9},{5... | collective-permute-start | bytes 3538952 | tf_op jit(solution)/shard_map/ppermute | solution.py:15
  445.1 40.0 %collective-permute-start.11 = (bf16[2,512,576]{1,2,0:T(8,128)(2,1)}, bf16[2,512,576]{1,2,0:T(8,128)(2,1)}, u32[]{:S(2)}, u32[]{:S(2)}) collective-permute-start(bf16[2,512,576]{1,2,0:T(8,128)(2,1)} %bitcast.512), channel_id=1, source_target_pairs={{0,8},{4,12},{8,0},{12,4},{16,24},{20,28},{24,16},{28,20},{1,9},{5... | collective-permute-start | bytes 3538952 | tf_op jit(solution)/shard_map/ppermute | solution.py:15
  450.1 204.1 %reduce-scatter.16.cloned.1.call-start = ((), (), s32[]{:S(2)}) async-start(), calls=%async_computation.8 | async-start | bytes 1622016
  508.3 271.1 %reduce-scatter.18.cloned.1.call-start = ((), (), s32[]{:S(2)}) async-start(), calls=%async_computation.9 | async-start | bytes 7299072
  526.5 394.2 %reduce-scatter.12.cloned.1.call-start = ((), (), s32[]{:S(2)}) async-start(), calls=%async_computation.6 | async-start | bytes 9732096 | tf_op jit(solution)/shard_map/reduce_scatter | solution.py:320
  538.2 524.2 %reduce-scatter.14.cloned.1.call-start = ((), (), s32[]{:S(2)}) async-start(), calls=%async_computation.7 | async-start | bytes 9732096 | tf_op jit(solution)/shard_map/reduce_scatter | solution.py:322
  (91 other events, 1303.5 us)
Sparse Core Ops, SparseCore 0:
  450.2 101.1 reduce-scatter.9
  558.1 96.1 reduce-scatter.15
  661.4 117.9 reduce-scatter.17
  785.8 134.8 reduce-scatter.11
  928.0 134.3 reduce-scatter.13
where the time goes:
time: 1080 us; the launch traced here: 1070 us
  waiting for transfers between devices  510 us (47%)
  local copies, waits for them, and re-layouts  193 us (18%)
  matrix products  181 us (17%)
  other arithmetic  106 us (10%)
  blocking collectives  41.9 us (4%)
  between operations  15.7 us (1%)
  starting transfers between devices  11.5 us (1%)
    unnamed x7, waiting for transfers between devices  176 us
    reduce_scatter x1, waiting for transfers between devices, on_device(): lax.psum_scatter(shrink_weight_grad, ('wide', 'narrow'), scatter_dimensio...  142 us
    reduce_scatter x1, waiting for transfers between devices, on_device(): lax.psum_scatter(expand_weight_grad, ('wide', 'narrow'), scatter_dimensio...  141 us
    ppermute x16, waiting for transfers between devices, partner(): lax.ppermute(shard, axis, [(i, i ^ 1 << apart) for i in range(lax.axis_si...  51.5 us
    another operation x16, other arithmetic, order_pair(): jnp.stack([own_part, their_part], axis_pos)  42.8 us
    unnamed x1, blocking collectives  41.9 us
    dot_general x1, matrix products, on_device(): jnp.dot(middle_low, expand_weight, preferred_element_type=float_type)  35 us
    dynamic_slice x20, local copies, waits for them, and re-layouts, select_half(): return lax.dynamic_index_in_dim(tensor, bit_value, axis_pos, keepdims=False)  33.4 us
  transfers between devices with their start and end apart: 21, of which 10 were waited for; matrix products, arithmetic and copies ran while one was open for 31% of the time, Pallas kernels for 0%

commit v1 on v0

v1 whole, which is shorter than its diff:
```python
import functools

import jax
import jax.numpy as jnp
from jax import lax
from jax.experimental import pallas as pl
from jax.experimental.pallas import tpu as pltpu
from jax.sharding import PartitionSpec as P

HEAD_DIM = 64
LANES = 128
EPS = 1e-05
QUAD = 4
F32 = jnp.float32
BF16 = jnp.bfloat16
BOTH = ("wide", "narrow")
ROOT_HALF = 0.7071067811865476
PHI_ZERO = 0.3989422804014327
VMEM_LIMIT = 56 << 20


def partner(shard, axis, flip):
    return lax.ppermute(shard, axis, [(i, i ^ flip) for i in range(lax.axis_size(axis))])


def pick(tensor, index, axis):
    return lax.dynamic_index_in_dim(tensor, index, axis, keepdims=False)


def after(value, *first):
    return lax.optimization_barrier((value,) + first)[0]


class Chain:
    def __init__(self, partial, turned=False):
        bits = {axis: lax.axis_size(axis).bit_length() - 1 for axis in BOTH}
        self.dims = [("wide", b) for b in reversed(range(bits["wide"]))]
        self.dims += [("narrow", b) for b in reversed(range(bits["narrow"]))]
        middle = [("wide", b) for b in range(1, bits["wide"])]
        self.steps = [("wide", 0)] + middle[:: -1 if turned else 1]
        self.steps += [("narrow", b) for b in range(bits["narrow"])]
        self.total = partial.reshape((2,) * len(self.dims) + (-1,) + partial.shape[1:])
        self.at = 0

    def launch(self):
        axis, bit = self.steps[self.at]
        self.mine = lax.axis_index(axis) // 2**bit % 2
        self.place = self.dims.index((axis, bit))
        away = pick(self.total, 1 - self.mine, self.place)
        self.arrived = partner(away, axis, 2**bit)
        return away

    def land(self):
        self.dims.pop(self.place)
        self.at += 1
        total = pick(self.total, self.mine, self.place).astype(F32) + self.arrived.astype(F32)
        self.total = total if self.at == len(self.steps) else total.astype(BF16)

    def step(self):
        self.land()
        return self.launch()

    def finish(self):
        self.land()
        while self.at < len(self.steps):
            self.launch()
            self.land()
        return self.total


def left_product(a, b):
    return lax.dot_general(a, b, (((0,), (0,)), ((), ())), preferred_element_type=F32)


def right_product(a, b):
    return lax.dot_general(a, b, (((1,), (1,)), ((), ())), preferred_element_type=F32)


def product(a, b):
    return jnp.dot(a, b, preferred_element_type=F32)


def norm_stats(values):
    row_mean = jnp.mean(values, axis=-1, keepdims=True)
    centered = values - row_mean
    spread = jnp.mean(centered * centered, axis=-1, keepdims=True)
    scale = lax.rsqrt(spread + EPS)
    return centered * scale, scale


def norm_back(grad, unit, scale, gain):
    inner = grad * gain
    first = jnp.mean(inner, axis=-1, keepdims=True)
    second = jnp.mean(inner * unit, axis=-1, keepdims=True)
    return scale * (inner - first - unit * second)


def column_sum(values):
    return jnp.sum(values, axis=0, keepdims=True)


def call(kernel, grid, scalars, ins, outs, arrays, scratch=(), aliases=None, flops=0, moved=0):
    return pl.pallas_call(
        kernel,
        grid_spec=pltpu.PrefetchScalarGridSpec(
            num_scalar_prefetch=len(scalars),
            grid=grid,
            in_specs=ins,
            out_specs=[o[0] for o in outs],
            scratch_shapes=list(scratch),
        ),
        out_shape=[o[1] for o in outs],
        input_output_aliases=aliases or {},
        compiler_params=pltpu.CompilerParams(vmem_limit_bytes=VMEM_LIMIT),
        cost_estimate=pl.CostEstimate(flops=flops, bytes_accessed=moved, transcendentals=0),
    )(*scalars, *arrays)


def whole(shape, once=True):
    mode = {"pipeline_mode": pl.Buffered(1)} if once else {}
    return pl.BlockSpec(shape, lambda *_: (0,) * len(shape), **mode)


def shaped(shape, dtype):
    return jax.ShapeDtypeStruct(shape, dtype)


def front_kernel(layout, spot, *refs):
    rows, spans = layout
    cut = rows[0] * spans[0]
    data, places = refs[:2], refs[2:6]
    gain, shift, weight, bias = refs[6:10]
    embedded_out, low_out, triple_out = refs[-3:]
    for at in range(2):
        tokens = data[at][...].astype(F32)
        width = tokens.shape[-1]
        parts = [tokens[:cut], tokens[cut:]]
        for which in range(2):
            place = places[2 * at + which][...].astype(F32)
            part = parts[which].reshape(rows[which], spans[which], width) + place[None]
            parts[which] = part.reshape(-1, width)
        embedded = jnp.concatenate(parts)
        embedded_out[at] = embedded
        unit, _ = norm_stats(embedded)
        base_low = (unit * gain[...] + shift[...]).astype(BF16)
        low_out[at] = base_low
        triple_out[at] = (product(base_low, weight[...]) + bias[...]).astype(BF16)


def front(layout, half, spot, data, table, gain, shift, weight, bias, earlier):
    rows, spans = layout
    tokens, width = data[0].shape
    triple = weight.shape[1]
    ins = [whole((tokens, width))] * 2
    for at in range(2):
        for span in spans:
            k = 2 * half + at
            ins.append(pl.BlockSpec((span, width), lambda i, s, k=k: (s[0] ^ k, 0)))
    ins += [whole((1, width))] * 2 + [whole((width, triple)), whole((1, triple))]
    ins += [pl.BlockSpec(memory_space=pl.ANY)] * len(earlier)
    outs = [
        (
            pl.BlockSpec((2, tokens, n), lambda i, s: (half, 0, 0)),
            shaped((QUAD, tokens, n), dtype),
        )
        for n, dtype in ((width, F32), (width, BF16), (triple, BF16))
    ]
    arrays = list(data) + [table] * 4 + [gain, shift, weight, bias] + list(earlier)
    return call(
        functools.partial(front_kernel, layout),
        (1,),
        [spot],
        ins,
        outs,
        arrays,
        aliases={1 + 10 + i: i for i in range(len(earlier))},
        flops=4 * tokens * width * triple,
        moved=2 * width * triple + 4 * tokens * (8 * width + triple),
    )


def head_rows(block, rows, span, at):
    part = block[:, at * span : (at + 1) * span, :] if rows > 1 else block
    return part.reshape(-1, part.shape[-1])


def first_head(shape):
    return lax.broadcasted_iota(jnp.int32, shape, len(shape) - 1) < HEAD_DIM


def attend_rows(query, key, value):
    first = first_head(query.shape)
    nothing = jnp.zeros_like(query)
    scaled = query * jnp.asarray(HEAD_DIM**-0.5, BF16)
    found = []
    for head in range(2):
        chosen = jnp.where(first, scaled, nothing) if head == 0 else jnp.where(first, nothing, scaled)
        scores = right_product(chosen, key)
        top = jnp.max(scores, axis=-1, keepdims=True)
        powers = jnp.exp(scores - top)
        share = 1.0 / jnp.sum(powers, axis=-1, keepdims=True)
        found.append(product((powers * share).astype(BF16), value))
    return jnp.where(first, found[0], found[1]).astype(BF16)


def attend_kernel(layout, query, key, value, out):
    rows, spans = layout
    for bucket in range(2):

        @pl.when(pl.program_id(1) == bucket)
        def _(bucket=bucket):
            blocks = [ref[...] for ref in (query, key, value)]
            for at in range(rows[bucket]):
                args = [head_rows(b, rows[bucket], spans[bucket], at) for b in blocks]
                result = attend_rows(*args).reshape(QUAD, spans[bucket], LANES)
                out[:, at * spans[bucket] : (at + 1) * spans[bucket], :] = result


def attend_flops(layout, pairs):
    rows, spans = layout
    return sum(2 * pairs * r * (QUAD * s) ** 2 * 2 * HEAD_DIM * 2 for r, s in zip(rows, spans))


def attend(layout, triple):
    rows, spans = layout
    tokens, width = triple.shape[1], triple.shape[2] // 3
    pairs = width // LANES
    size = rows[0] * spans[0]
    ins = [
        pl.BlockSpec((QUAD, size, LANES), lambda p, b, w=w: (0, b, w * pairs + p)) for w in range(3)
    ]
    outs = [
        (
            pl.BlockSpec((QUAD, size, LANES), lambda p, b: (0, b, p)),
            shaped((QUAD, tokens, width), BF16),
        )
    ]
    return call(
        functools.partial(attend_kernel, layout),
        (pairs, 2),
        [],
        ins,
        outs,
        [triple] * 3,
        flops=attend_flops(layout, pairs),
        moved=QUAD * tokens * width * 8,
    )[0]


def attend_back_rows(query, key, value, grad):
    first = first_head(query.shape)
    nothing = jnp.zeros_like(query)
    scaled = query * jnp.asarray(HEAD_DIM**-0.5, BF16)
    query_grads, key_grads, value_grads = [], [], []
    for head in range(2):
        def only(array):
            return jnp.where(first, array, nothing) if head == 0 else jnp.where(first, nothing, array)

        scores = right_product(key, only(scaled))
        top = jnp.max(scores, axis=0, keepdims=True)
        powers = jnp.exp(scores - top)
        soft = powers * (1.0 / jnp.sum(powers, axis=0, keepdims=True))
        prob_grad = right_product(value, only(grad))
        inner = jnp.sum(soft * prob_grad, axis=0, keepdims=True)
        score_grad = (soft * (prob_grad - inner)).astype(BF16)
        value_grads.append(product(soft.astype(BF16), grad))
        key_grads.append(product(score_grad, scaled))
        query_grads.append(left_product(score_grad, key) * HEAD_DIM**-0.5)
    return [
        jnp.where(first, two[0], two[1]).astype(BF16) for two in (query_grads, key_grads, value_grads)
    ]


def attend_back_kernel(layout, bucket, query, key, value, grad, *rest):
    rows, spans = layout[0][bucket], layout[1][bucket]
    outs = rest[-3:]
    blocks = [ref[...] for ref in (query, key, value, grad)]
    for at in range(rows):
        args = [head_rows(b, rows, spans, at) for b in blocks]
        for ref, result in zip(outs, attend_back_rows(*args)):
            ref[:, at * spans : (at + 1) * spans, :] = result.reshape(QUAD, spans, LANES)


def attend_back(layout, bucket, triple, grad, earlier):
    rows, spans = layout
    tokens, width = triple.shape[1], triple.shape[2] // 3
    pairs = width // LANES
    size = rows[0] * spans[0]
    ins = [
        pl.BlockSpec((QUAD, size, LANES), lambda p, w=w: (0, bucket, w * pairs + p)) for w in range(3)
    ]
    one = pl.BlockSpec((QUAD, size, LANES), lambda p: (0, bucket, p))
    ins += [one] + [pl.BlockSpec(memory_space=pl.ANY)] * len(earlier)
    outs = [(one, shaped((QUAD, tokens, width), BF16))] * 3
    return call(
        functools.partial(attend_back_kernel, layout, bucket),
        (pairs,),
        [],
        ins,
        outs,
        [triple] * 3 + [grad] + list(earlier),
        aliases={4 + i: i for i in range(len(earlier))},
        flops=int(2.5 * attend_flops((rows[bucket : bucket + 1], spans[bucket : bucket + 1]), pairs)),
        moved=QUAD * size * width * 14,
    )


def alive_rows(limits, size, count):
    at = lax.broadcasted_iota(jnp.int32, (count, 1), 0)
    short = (at < limits[0]).astype(F32)
    long = (at >= size).astype(F32) * (at < limits[1]).astype(F32)
    return short + long


def ahead_kernel(size, chunk, limits, *refs):
    (context, embedded, cotangent, embed_gain, embed_shift, project_out, output_bias) = refs[:7]
    (middle_gain, middle_shift, expand, expand_bias, shrink, shrink_bias, gain, shift) = refs[7:15]
    (output, inner_out, middle_out, active_out, slope_out, grad_out, grad_low_out, sums) = refs[15:]
    unit, _ = norm_stats(embedded[0])
    inner = unit * embed_gain[...] + embed_shift[...]
    inner = inner + (product(context[0], project_out[...]) + output_bias[...])
    inner_out[0] = inner
    unit, _ = norm_stats(inner)
    middle = unit * middle_gain[...] + middle_shift[...]
    middle_low = middle.astype(BF16)
    middle_out[0] = middle_low
    hidden = expand.shape[1]
    total = middle + shrink_bias[...]
    for start in range(0, hidden, chunk):
        part = slice(start, start + chunk)
        expanded = product(middle_low, expand[:, part]) + expand_bias[:, part]
        below = 0.5 + 0.5 * lax.erf(expanded * ROOT_HALF)
        active = (expanded * below).astype(BF16)
        active_out[0, :, part] = active
        density = jnp.exp(expanded * expanded * -0.5) * PHI_ZERO
        slope_out[0, :, part] = (below + expanded * density).astype(BF16)
        total = total + product(active, shrink[part, :])
    unit, scale = norm_stats(total)
    alive = alive_rows(limits, size, unit.shape[0])
    result = unit * gain[...] + shift[...]
    output[0] = (result * alive).astype(BF16)
    upstream = cotangent[0].astype(F32) * alive
    grad = norm_back(upstream, unit, scale, gain[...])
    grad_low = grad.astype(BF16)
    grad_out[0] = grad
    grad_low_out[0] = grad_low
    found = [column_sum(upstream * unit), column_sum(upstream), column_sum(grad_low.astype(F32))]

    @pl.when(pl.program_id(0) == 0)
    def _():
        sums[...] = jnp.zeros_like(sums)

    for at, value in enumerate(found):
        sums[at : at + 1, :] += value


def ahead(size, limits, context, embedded, cotangent, weights):
    pieces, tokens, width = context.shape
    hidden = weights[6].shape[1]
    row = pl.BlockSpec((1, tokens, width), lambda i, s: (i, 0, 0))
    wide = pl.BlockSpec((1, tokens, hidden), lambda i, s: (i, 0, 0))
    ins = [row] * 3 + [whole(w.shape) for w in weights]
    outs = [(row, shaped((pieces, tokens, width), dtype)) for dtype in (BF16, F32, BF16)]
    outs += [(wide, shaped((pieces, tokens, hidden), BF16))] * 2
    outs += [(row, shaped((pieces, tokens, width), dtype)) for dtype in (F32, BF16)]
    outs += [(whole((8, width), False), shaped((8, width), F32))]
    return call(
        functools.partial(ahead_kernel, size, width),
        (pieces,),
        [limits],
        ins,
        outs,
        [context, embedded, cotangent] + list(weights),
        flops=2 * pieces * tokens * width * (width + 2 * hidden),
        moved=4 * width * hidden + pieces * tokens * (24 * width + 4 * hidden),
    )


def behind_kernel(chunk, *refs):
    grad_low, slope, grad, inner, shrink, expand, project_out, middle_gain = refs[:8]
    expanded_out, mixed_out, mixed_low_out, context_out, sums, bias_sums = refs[8:]

    @pl.when(pl.program_id(0) == 0)
    def _():
        sums[...] = jnp.zeros_like(sums)
        bias_sums[...] = jnp.zeros_like(bias_sums)

    hidden = expand.shape[1]
    total = grad[0]
    for start in range(0, hidden, chunk):
        part = slice(start, start + chunk)
        raised = right_product(grad_low[0], shrink[part, :]) * slope[0, :, part].astype(F32)
        low = raised.astype(BF16)
        expanded_out[0, :, part] = low
        bias_sums[:, part] += column_sum(low.astype(F32))
        total = total + right_product(low, expand[:, part])
    unit, scale = norm_stats(inner[0])
    mixed = norm_back(total, unit, scale, middle_gain[...])
    mixed_low = mixed.astype(BF16)
    mixed_out[0] = mixed
    mixed_low_out[0] = mixed_low
    context_out[0] = right_product(mixed_low, project_out[...]).astype(BF16)
    found = [column_sum(total * unit), column_sum(total), column_sum(mixed_low.astype(F32))]
    for at, value in enumerate(found):
        sums[at : at + 1, :] += value


def behind(grad_low, slope, grad, inner, shrink, expand, project_out, middle_gain):
    pieces, tokens, width = grad.shape
    hidden = expand.shape[1]
    row = pl.BlockSpec((1, tokens, width), lambda i: (i, 0, 0))
    wide = pl.BlockSpec((1, tokens, hidden), lambda i: (i, 0, 0))
    weights = [shrink, expand, project_out, middle_gain]
    ins = [row, wide, row, row] + [whole(w.shape) for w in weights]
    outs = [(wide, shaped((pieces, tokens, hidden), BF16))]
    outs += [(row, shaped((pieces, tokens, width), dtype)) for dtype in (F32, BF16, BF16)]
    outs += [(whole((8, width), False), shaped((8, width), F32))]
    outs += [(whole((1, hidden), False), shaped((1, hidden), F32))]
    return call(
        functools.partial(behind_kernel, width),
        (pieces,),
        [],
        ins,
        outs,
        [grad_low, slope, grad, inner] + weights,
        flops=2 * pieces * tokens * width * (width + 2 * hidden),
        moved=4 * width * hidden + pieces * tokens * (18 * width + 4 * hidden),
    )


def last_kernel(layout, spot, *refs):
    rows, spans = layout
    cut = rows[0] * spans[0]
    query, key, value, mixed, embedded, weight, gain = refs[:7]
    input_out, short_out, long_out, sums = refs[7:]
    width = mixed.shape[-1]
    total = mixed[0]
    for at, ref in enumerate((query, key, value)):
        total = total + right_product(ref[0], weight[:, at * width : (at + 1) * width])
    unit, scale = norm_stats(embedded[0])
    grad = norm_back(total, unit, scale, gain[...])
    input_out[0] = grad.astype(BF16)
    short_out[...] = jnp.sum(grad[:cut].reshape(rows[0], spans[0], width), axis=0)
    long_out[...] = jnp.sum(grad[cut:].reshape(rows[1], spans[1], width), axis=0)
    found = [
        column_sum(total * unit),
        column_sum(total),
        column_sum(query[0].astype(F32)),
        column_sum(value[0].astype(F32)),
    ]

    @pl.when(pl.program_id(0) == 0)
    def _():
        sums[...] = jnp.zeros_like(sums)

    for at, item in enumerate(found):
        sums[at : at + 1, :] += item


def last(layout, spot, grads, mixed, embedded, weight, gain):
    rows, spans = layout
    pieces, tokens, width = mixed.shape
    row = pl.BlockSpec((1, tokens, width), lambda i, s: (i, 0, 0))
    ins = [row] * 5 + [whole(weight.shape), whole(gain.shape)]
    outs = [(row, shaped((pieces, tokens, width), BF16))]
    outs += [
        (
            pl.BlockSpec((span, width), lambda i, s: (s[0] ^ i, 0)),
            shaped((QUAD * span, width), F32),
        )
        for span in spans
    ]
    outs += [(whole((8, width), False), shaped((8, width), F32))]
    return call(
        functools.partial(last_kernel, layout),
        (pieces,),
        [spot],
        ins,
        outs,
        list(grads) + [mixed, embedded, weight, gain],
        flops=6 * pieces * tokens * width * width,
        moved=6 * width * width + pieces * tokens * 18 * width,
    )


def send_pieces(short, long, spot):
    width = short.shape[-1]
    parts = [a.reshape(QUAD, -1, width) for a in (short, long)]
    pieces = []
    for k in range(QUAD):
        piece = jnp.concatenate([pick(a, spot ^ k, 0) for a in parts])
        pieces.append(piece if k == 0 else partner(piece, "wide", k))
    return pieces


def return_pieces(pieces, size, spot):
    homes = [jnp.zeros((QUAD,) + p.shape[1:], p.dtype) for p in (pieces[:, :size], pieces[:, size:])]
    for k in range(QUAD):
        piece = pieces[k] if k == 0 else partner(pieces[k], "wide", k)
        for at, part in enumerate((piece[:size], piece[size:])):
            homes[at] = lax.dynamic_update_index_in_dim(homes[at], part, spot ^ k, 0)
    return homes


def on_device(
    short_input,
    long_input,
    short_cotangent,
    long_cotangent,
    short_live,
    long_live,
    position_table,
    embed_gain,
    embed_shift,
    project_in,
    query_bias,
    value_bias,
    project_out,
    output_bias,
    middle_gain,
    middle_shift,
    expand_weight,
    expand_bias,
    shrink_weight,
    shrink_bias,
    final_gain,
    final_shift,
):
    width = short_input.shape[-1]
    spot = lax.axis_index("wide") % QUAD
    group = lax.axis_index("wide") // QUAD * lax.axis_size("narrow") + lax.axis_index("narrow")
    rows = (short_input.shape[1] // QUAD, long_input.shape[1] // QUAD)
    spans = (short_input.shape[2], long_input.shape[2])
    layout = (rows, spans)
    size = rows[0] * spans[0]
    assert size == rows[1] * spans[1]
    spots = jnp.asarray(spot, jnp.int32).reshape(1)
    alive = [
        jnp.clip(pick(live, group, 0) - spot * r, 0, r) * s
        for live, r, s in zip((short_live, long_live), rows, spans)
    ]
    limits = jnp.stack([alive[0], size + alive[1]]).astype(jnp.int32)

    def line(*vectors):
        return jnp.concatenate(vectors).astype(F32)[None]

    pieces = send_pieces(short_input, long_input, spot)
    cotangent = jnp.stack(send_pieces(short_cotangent, long_cotangent, spot))
    embed_lines = (line(embed_gain), line(embed_shift))
    bias_line = line(query_bias, jnp.zeros_like(query_bias), value_bias)
    found = ()
    for half in range(2):
        found = front(
            layout,
            half,
            spots,
            pieces[2 * half : 2 * half + 2],
            position_table,
            *embed_lines,
            project_in,
            bias_line,
            found,
        )
    embedded, base_low, triple = found
    context = attend(layout, triple)
    weights = embed_lines + (
        project_out,
        line(output_bias),
        line(middle_gain),
        line(middle_shift),
        expand_weight,
        line(expand_bias),
        shrink_weight,
        line(shrink_bias),
        line(final_gain),
        line(final_shift),
    )
    output, inner, middle_low, active, slope, grad, grad_low, final_sums = ahead(
        size, limits, context, embedded, cotangent, weights
    )
    flat = lambda a: a.reshape(-1, a.shape[-1])
    shrink_chain = Chain(left_product(flat(active), flat(grad_low)).astype(BF16))
    sent = shrink_chain.launch()
    expanded_low, mixed, mixed_low, context_grad, middle_sums, expand_sums = behind(
        after(grad_low, sent), slope, grad, inner, shrink_weight, expand_weight, project_out, line(middle_gain)
    )
    expand_chain = Chain(left_product(flat(middle_low), flat(expanded_low)).astype(BF16), True)
    out_chain = Chain(left_product(flat(context), flat(mixed_low)).astype(BF16), True)
    sent = [expand_chain.launch(), out_chain.launch(), shrink_chain.step()]
    grads = attend_back(layout, 0, triple, after(context_grad, *sent), ())
    sent = [expand_chain.step(), out_chain.step()]
    grads = attend_back(layout, 1, triple, after(context_grad, *sent, grads[0]), grads)
    in_parts = [left_product(flat(base_low), flat(g)).astype(BF16) for g in grads]
    in_chains = [
        Chain(jnp.concatenate([in_parts[0], in_parts[1][:, : width // 2]], axis=1)),
        Chain(jnp.concatenate([in_parts[1][:, width // 2 :], in_parts[2]], axis=1), True),
    ]
    sent = [c.launch() for c in in_chains] + [shrink_chain.step()]
    input_grad, short_sum, long_sum, embed_sums = last(
        layout, spots, grads, after(mixed, *sent), embedded, project_in, embed_lines[0]
    )
    position = jnp.concatenate([long_sum[: short_sum.shape[0]] + short_sum, long_sum[short_sum.shape[0] :]])
    hidden = expand_weight.shape[1]
    vectors = jnp.concatenate(
        [
            embed_sums[:4],
            final_sums[:3],
            middle_sums[:3],
            jnp.zeros((LANES - 10, width), F32),
        ]
    )
    spread = expand_sums.reshape(width, hidden // width)
    tail = jnp.concatenate([position, vectors]).T
    tail = lax.dynamic_update_slice_in_dim(tail, spread, position.shape[0] + 10, 1)
    tail_chain = Chain(tail.astype(BF16), True)
    tail_chain.launch()
    outputs = return_pieces(output, size, spot)
    input_grads = return_pieces(input_grad, size, spot)
    shrink_grad = shrink_chain.finish()
    expand_grad = expand_chain.finish()
    out_grad = out_chain.finish()
    in_grad = jnp.concatenate([c.finish() for c in in_chains], axis=1)
    tail_sum = tail_chain.finish()
    length = position.shape[0]
    position_grad = tail_sum[:, :length].T
    vector = [tail_sum[:, length + i] for i in range(10)]
    expand_bias_grad = tail_sum[:, length + 10 : length + 10 + hidden // width].reshape(-1)
    return (
        outputs[0].reshape(short_input.shape),
        outputs[1].reshape(long_input.shape),
        input_grads[0].reshape(short_input.shape),
        input_grads[1].reshape(long_input.shape),
        position_grad,
        vector[0],
        vector[1],
        in_grad,
        vector[2],
        vector[3],
        out_grad,
        vector[9],
        vector[7],
        vector[8],
        expand_grad,
        expand_bias_grad,
        shrink_grad,
        vector[6],
        vector[4],
        vector[5],
    )


def solution(mesh):
    rows = P(BOTH, None, None, None)
    vector, matrix = P(BOTH), P(BOTH, None)
    in_specs = (rows,) * 4 + (P(),) * 18
    out_specs = (rows,) * 4 + (
        P(None, BOTH),
        vector,
        vector,
        matrix,
        vector,
        vector,
        matrix,
        vector,
        vector,
        vector,
        matrix,
        vector,
        matrix,
        vector,
        vector,
        vector,
    )
    return jax.shard_map(on_device, mesh=mesh, in_specs=in_specs, out_specs=out_specs, check_vma=False)
```

time: 1080 us -> 369 us (0.34)
  waiting for transfers between devices: 510 us -> 84.5 us
  matrix products: 181 us -> 24.7 us
  local copies, waits for them, and re-layouts: 193 us -> 57 us
  Pallas kernels: 0 us -> 127 us
  other arithmetic: 106 us -> 26.1 us
  blocking collectives: 41.9 us -> 0 us
  starting transfers between devices: 11.5 us -> 40.3 us
  between operations: 15.7 us -> 3.16 us
    reduce_scatter x3 -> x0, waiting for transfers between devices: 283 us -> none  [the longest x1 142 us: on_device(): lax.psum_scatter(shrink_weight_grad, ('wide', 'narrow'), scatter_dimensio...]
    unnamed x7 -> x0, waiting for transfers between devices: 176 us -> none
    dot_general x30 -> x6, matrix products: 181 us -> 24.7 us  [left_product(): lax.dot_general(a, b, (((0,), (0,)), ((), ())), preferred_element_type=F32)]
    pallas_call x0 -> x8, Pallas kernels: none -> 127 us  [call(): pl.pallas_call(kernel, grid_spec=pltpu.PrefetchScalarGridSpec(num_scalar_...]
    another operation x20 -> x2, local copies, waits for them, and re-layouts: 59.6 us -> 0.11 us
    another operation x18 -> x3, other arithmetic: 44.4 us -> 1.96 us  [the longest x2 1.37 us: on_device(): cotangent = jnp.stack(send_pieces(short_cotangent, long_cotangent, spot))]
    unnamed x1 -> x0, blocking collectives: 41.9 us -> none
    ppermute x16 -> x42, waiting for transfers between devices: 51.5 us -> 84.5 us  [partner(): lax.ppermute(shard, axis, [(i, i ^ flip) for i in range(lax.axis_size(axi...]
  transfers between devices with their start and end apart: 21 -> 42, of which waited for: 10 -> 19; matrix products, arithmetic and copies ran while one was open for 31% -> 24% of each run, Pallas kernels for 0% -> 28%
where the time goes in v1:
time: 369 us; the launch traced here: 363 us
  Pallas kernels  127 us (34%)
  waiting for transfers between devices  84.5 us (23%)
  local copies, waits for them, and re-layouts  57 us (15%)
  starting transfers between devices  40.3 us (11%)
  other arithmetic  26.1 us (7%)
  matrix products  24.7 us (7%)
    pallas_call x8, Pallas kernels, call(): pl.pallas_call(kernel, grid_spec=pltpu.PrefetchScalarGridSpec(num_scalar_...  127 us
    ppermute x42, waiting for transfers between devices, partner(): lax.ppermute(shard, axis, [(i, i ^ flip) for i in range(lax.axis_size(axi...  84.5 us
    ppermute x42, starting transfers between devices, partner(): lax.ppermute(shard, axis, [(i, i ^ flip) for i in range(lax.axis_size(axi...  40.3 us
    dot_general x6, matrix products, left_product(): lax.dot_general(a, b, (((0,), (0,)), ((), ())), preferred_element_type=F32)  24.7 us
    convert_element_type x24, other arithmetic, land(): self.total = total if self.at == len(self.steps) else total.astype(BF16)  13.8 us
    dynamic_slice x10, local copies, waits for them, and re-layouts, pick(): return lax.dynamic_index_in_dim(tensor, index, axis, keepdims=False)  10.6 us
    squeeze x28, local copies, waits for them, and re-layouts, pick(): return lax.dynamic_index_in_dim(tensor, index, axis, keepdims=False)  10.1 us
    broadcast_in_dim x8, local copies, waits for them, and re-layouts, line(): return jnp.concatenate(vectors).astype(F32)[None]  8.74 us
  transfers between devices with their start and end apart: 42, of which 19 were waited for; matrix products, arithmetic and copies ran while one was open for 24% of the time, Pallas kernels for 28%

profile of v1, /device:TPU:0, one launch (start us, length us, event | category | flops | bytes accessed | tf_op | source)
XLA Modules:
  0.0 363.2 jit_solution(8734045633735241552)
XLA Ops:
  25.0 6.1 %shard_map.365 = (f32[4,256,768]{2,1,0:T(8,128)}, bf16[4,256,768]{2,1,0:T(8,128)(2,1)}, bf16[4,256,2304]{2,1,0:T(8,128)(2,1)}) custom-call(s32[1]{0:T(128)} %bitcast.4.spot, bf16[256,768]{1,0:T(8,128)(2,1)} %pad_maximum_fusion.5.refs_0_, bf16[256,768]{1,0:T(8,128)(2,1)} %copy-done.23, bf16[512,768]{1,0:T(8,128)(2,1)} %refs_5_.6, bf16[512,768]{1,0:T(8,128)(2,1)} %refs_5_.6, ...), custom_call_target="tpu_custom_call" | custom-call | flops 1811939328 | bytes 12189696 | tf_op jit(solution)/shard_map/pallas_call | solution.py:103
  31.1 6.2 %shard_map.366 = (f32[4,256,768]{2,1,0:T(8,128)}, bf16[4,256,768]{2,1,0:T(8,128)(2,1)}, bf16[4,256,2304]{2,1,0:T(8,128)(2,1)}) custom-call(s32[1]{0:T(128)} %bitcast.4.spot, bf16[256,768]{1,0:T(8,128)(2,1)} %collective-permute-done.refs_0_, ...), custom_call_target="tpu_custom_call", output_to_operand_aliasing={{0}: (11, {}), {1}: (12, {}), {2}: (13, {})} | custom-call | flops 1811939328 | bytes 12189696 | tf_op jit(solution)/shard_map/pallas_call | solution.py:103
  37.3 26.4 %shard_map.367.refs_0_ = bf16[4,256,768]{2,1,0:T(8,128)(2,1)} custom-call(bf16[4,256,2304]{2,1,0:T(8,128)(2,1)} %get-tuple-element.57.query.key.value, bf16[4,256,2304]{2,1,0:T(8,128)(2,1)} %get-tuple-element.57.query.key.value, bf16[4,256,2304]{2,1,0:T(8,128)(2,1)} %get-tuple-element.57.query.key.value), custom_call_target="tpu_custom_call" | custom-call | flops 1006632960 | bytes 6291456 | tf_op jit(solution)/shard_map/pallas_call | solution.py:103
  65.0 26.7 %shard_map.368 = (bf16[4,256,768]{2,1,0:T(8,128)(2,1)}, f32[4,256,768]{2,1,0:T(8,128)}, bf16[4,256,768]{2,1,0:T(8,128)(2,1)}, bf16[4,256,3072]{2,1,0:T(8,128)(2,...) custom-call(s32[2]{0:T(128)} %pad_add_fusion.limits, ...), custom_call_target="tpu_custom_call" | custom-call | flops 10871635968 | bytes 40894464 | tf_op jit(solution)/shard_map/pallas_call | solution.py:103
  91.7 7.7 %bitcast_convert_fusion.1 = bf16[3072,768]{1,0:T(8,128)(2,1)S(1)} fusion(bf16[4,256,3072]{2,1,0:T(8,128)(2,1)} %get-tuple-element.61, bf16[4,256,768]{2,1,0:T(8,128)(2,1)} %get-tuple-element.62.refs_0_), kind=kOutput, calls=%fused_computation.1 | convolution fusion | flops 4834197504 | bytes 12582912 | tf_op jit(solution)/shard_map/dot_general | solution.py:72
  101.6 20.6 %shard_map.369 = (bf16[4,256,3072]{2,1,0:T(8,128)(2,1)}, f32[4,256,768]{2,1,0:T(8,128)}, bf16[4,256,768]{2,1,0:T(8,128)(2,1)}, bf16[4,256,768]{2,1,0:T(8,128)(2,...) custom-call(bf16[4,256,768]{2,1,0:T(8,128)(2,1)} %get-tuple-element.62.refs_0_, ...), custom_call_target="tpu_custom_call" | custom-call | flops 10871635968 | bytes 36175872 | tf_op jit(solution)/shard_map/pallas_call | solution.py:103
  122.2 8.2 %bitcast_convert_fusion = bf16[768,3072]{1,0:T(8,128)(2,1)S(1)} fusion(bf16[4,256,768]{2,1,0:T(8,128)(2,1)S(1)} %copy-done.32, bf16[4,256,3072]{2,1,0:T(8,128)(2,1)} %get-tuple-element.68), kind=kOutput, calls=%fused_computation | convolution fusion | flops 4834197504 | bytes 12582912 | tf_op jit(solution)/shard_map/dot_general | solution.py:72
  149.7 5.3 %collective-permute-done.7 = bf16[256,768]{1,0:T(8,128)(2,1)S(1)} collective-permute-done((bf16[256,768]{1,0:T(8,128)(2,1)S(1)}, bf16[256,768]{1,0:T(8,128)(2,1)S(1)}, u32[]{:S(2)}, u32[]{:S(2)}) %collective-permute-start.7) | collective-permute-done | bytes 393248 | tf_op jit(solution)/shard_map/ppermute | solution.py:23
  159.1 3.2 collective-permute-done.8
  162.3 3.7 %collective-permute-done.32 = bf16[2,2,24,768]{3,2,0,1:T(8,128)(2,1)S(1)} collective-permute-done((bf16[2,2,24,768]{3,2,0,1:T(8,128)(2,1)S(1)}, bf16[2,2,24,768]{3,2,0,1:T(8,128)(2,1)S(1)}, u32[]{:S(2)}, u32[]{:S(2)}) %collective-permute-start.32) | collective-permute-done | bytes 147488 | tf_op jit(solution)/shard_map/ppermute | solution.py:23
  167.7 2.8 collective-permute-done.33
  182.2 15.5 %shard_map.370 = (bf16[4,256,768]{2,1,0:T(8,128)(2,1)}, bf16[4,256,768]{2,1,0:T(8,128)(2,1)}, bf16[4,256,768]{2,1,0:T(8,128)(2,1)}) custom-call(bf16[4,256,2304]{2,1,0:T(8,128)(2,1)} %get-tuple-element.57.query.key.value, bf16[4,256,2304]{2,1,0:T(8,128)(2,1)} %get-tuple-element.57.query.key.value, bf16[4,256,2304]{2,1,0:T(8,128)(2,1)} %get-tuple-element.57.query.key.value, ...), custom_call_target="tpu_custom_call" | custom-call | flops 503316480 | bytes 5505024 | tf_op jit(solution)/shard_map/pallas_call | solution.py:103
  197.7 15.1 %shard_map.371 = (bf16[4,256,768]{2,1,0:T(8,128)(2,1)}, bf16[4,256,768]{2,1,0:T(8,128)(2,1)}, bf16[4,256,768]{2,1,0:T(8,128)(2,1)}) custom-call(bf16[4,256,2304]{2,1,0:T(8,128)(2,1)} %get-tuple-element.57.query.key.value, bf16[4,256,2304]{2,1,0:T(8,128)(2,1)} %get-tuple-element.57.query.key.value, ...), custom_call_target="tpu_custom_call", output_to_operand_aliasing={{0}: (4, {}), {1}: (5, {}), {2}: (6, {})} | custom-call | flops 2013265920 | bytes 5505024 | tf_op jit(solution)/shard_map/pallas_call | solution.py:103
  212.9 3.0 bitcast_convert_fusion.4
  218.8 3.9 %copy.77 = bf16[768,1152]{1,0:T(8,128)(2,1)} copy(bf16[768,1152]{0,1:T(8,128)(2,1)} %pad_maximum_fusion) | data formatting | bytes 3538944 | tf_op jit(solution)/shard_map/concatenate | solution.py:595
  225.0 2.9 bitcast_convert_fusion.2
  229.2 3.9 %copy.79 = bf16[768,1152]{1,0:T(8,128)(2,1)} copy(bf16[768,1152]{0,1:T(8,128)(2,1)} %pad_maximum_fusion.1) | data formatting | bytes 3538944 | tf_op jit(solution)/shard_map/concatenate | solution.py:596
  243.5 21.4 %collective-permute-done.12 = bf16[2,2,2,96,768]{4,3,1,2,0:T(8,128)(2,1)S(1)} collective-permute-done((bf16[2,2,2,96,768]{4,3,1,2,0:T(8,128)(2,1)S(1)}, bf16[2,2,2,96,768]{4,3,1,2,0:T(8,128)(2,1)S(1)}, u32[]{:S(2)}, u32[]{:S(2)}) %collective-permute-start.12) | collective-permute-done | bytes 1179680 | tf_op jit(solution)/shard_map/ppermute | solution.py:23
  271.2 10.9 %shard_map.372 = (bf16[4,256,768]{2,1,0:T(8,128)(2,1)}, f32[128,768]{1,0:T(8,128)}, f32[512,768]{1,0:T(8,128)}, f32[8,768]{1,0:T(8,128)}) custom-call(s32[1]{0:T(128)} %bitcast.4.spot, bf16[4,256,768]{2,1,0:T(8,128)(2,1)} %get-tuple-element.75.refs_0_, bf16[4,256,768]{2,1,0:T(8,128)(2,1)} %get-tuple-element.76.refs_1_, ...), custom_call_target="tpu_custom_call" | custom-call | flops 3623878656 | bytes 17694720 | tf_op jit(solution)/shard_map/pallas_call | solution.py:103
  292.7 5.2 %collective-permute-done.23 = bf16[2,2,24,1152]{3,2,1,0:T(8,128)(2,1)S(1)} collective-permute-done((bf16[2,2,24,1152]{3,2,1,0:T(8,128)(2,1)S(1)}, bf16[2,2,24,1152]{3,2,1,0:T(8,128)(2,1)S(1)}, u32[]{:S(2)}, u32[]{:S(2)}) %collective-permute-start.23) | collective-permute-done | bytes 221216 | tf_op jit(solution)/shard_map/ppermute | solution.py:23
  298.9 5.1 %collective-permute-done.28 = bf16[2,2,24,1152]{3,2,0,1:T(8,128)(2,1)S(1)} collective-permute-done((bf16[2,2,24,1152]{3,2,0,1:T(8,128)(2,1)S(1)}, bf16[2,2,24,1152]{3,2,0,1:T(8,128)(2,1)S(1)}, u32[]{:S(2)}, u32[]{:S(2)}) %collective-permute-start.28) | collective-permute-done | bytes 221216 | tf_op jit(solution)/shard_map/ppermute | solution.py:23
  305.0 10.9 %collective-permute-done.14 = bf16[256,768]{1,0:T(8,128)(2,1)S(1)} collective-permute-done((bf16[256,768]{1,0:T(8,128)(2,1)S(1)}, bf16[256,768]{1,0:T(8,128)(2,1)S(1)}, u32[]{:S(2)}, u32[]{:S(2)}) %collective-permute-start.14) | collective-permute-done | bytes 393248 | tf_op jit(solution)/shard_map/ppermute | solution.py:23
  321.3 3.2 collective-permute-done.29
  343.9 7.1 %collective-permute-done.37 = bf16[2,24,3072]{2,1,0:T(8,128)(2,1)S(1)} collective-permute-done((bf16[2,24,3072]{2,1,0:T(8,128)(2,1)S(1)}, bf16[2,24,3072]{2,1,0:T(8,128)(2,1)S(1)}, u32[]{:S(2)}, u32[]{:S(2)}) %collective-permute-start.37) | collective-permute-done | bytes 294944 | tf_op jit(solution)/shard_map/ppermute | solution.py:23
  (277 shorter events, 135.1 us)
Async XLA Ops:
  3.5 20.7 %collective-permute-start.2 = (bf16[256,768]{1,0:T(8,128)(2,1)}, bf16[256,768]{1,0:T(8,128)(2,1)S(1)}, u32[]{:S(2)}, u32[]{:S(2)}) collective-permute-start(bf16[256,768]{1,0:T(8,128)(2,1)} %pad_maximum_fusion.6), channel_id=1, source_target_pairs={{0,4},{4,0},{8,12},{12,8},{16,20},{20,16},{24,28},{28,24},{1,5},{5... | collective-permute-start | bytes 1179656 | tf_op jit(solution)/shard_map/ppermute | solution.py:23
  4.0 27.1 %collective-permute-start.1 = (bf16[256,768]{1,0:T(8,128)(2,1)S(1)}, bf16[256,768]{1,0:T(8,128)(2,1)}, u32[]{:S(2)}, u32[]{:S(2)}) collective-permute-start(bf16[256,768]{1,0:T(8,128)(2,1)S(1)} %pad_maximum_fusion.4), channel_id=1, source_target_pairs={{0,12},{4,8},{8,4},{12,0},{16,28},{20,24},{24,20},{28,16},{1,13},{... | collective-permute-start | bytes 1179656 | tf_op jit(solution)/shard_map/ppermute | solution.py:23
  6.7 24.4 %collective-permute-start = (bf16[256,768]{1,0:T(8,128)(2,1)S(1)}, bf16[256,768]{1,0:T(8,128)(2,1)}, u32[]{:S(2)}, u32[]{:S(2)}) collective-permute-start(bf16[256,768]{1,0:T(8,128)(2,1)S(1)} %pad_maximum_fusion.3), channel_id=1, source_target_pairs={{0,8},{4,12},{8,0},{12,4},{16,24},{20,28},{24,16},{28,20},{1,9},{5... | collective-permute-start | bytes 1179656 | tf_op jit(solution)/shard_map/ppermute | solution.py:23
  6.8 56.8 %collective-permute-start.3 = (bf16[256,768]{1,0:T(8,128)(2,1)S(1)}, bf16[256,768]{1,0:T(8,128)(2,1)S(1)}, u32[]{:S(2)}, u32[]{:S(2)}) collective-permute-start(bf16[256,768]{1,0:T(8,128)(2,1)S(1)} %pad_maximum_fusion.7), channel_id=1, source_target_pairs={{0,4},{4,0},{8,12},{12,8},{16,20},{20,16},{24,28},{28,24},{1,5},{5... | collective-permute-start | bytes 1179656 | tf_op jit(solution)/shard_map/ppermute | solution.py:23
  7.1 56.6 %collective-permute-start.4 = (bf16[256,768]{1,0:T(8,128)(2,1)S(1)}, bf16[256,768]{1,0:T(8,128)(2,1)S(1)}, u32[]{:S(2)}, u32[]{:S(2)}) collective-permute-start(bf16[256,768]{1,0:T(8,128)(2,1)S(1)} %pad_maximum_fusion.8), channel_id=1, source_target_pairs={{0,8},{4,12},{8,0},{12,4},{16,24},{20,28},{24,16},{28,20},{1,9},{5... | collective-permute-start | bytes 1179656 | tf_op jit(solution)/shard_map/ppermute | solution.py:23
  24.3 39.4 %collective-permute-start.5 = (bf16[256,768]{1,0:T(8,128)(2,1)S(1)}, bf16[256,768]{1,0:T(8,128)(2,1)S(1)}, u32[]{:S(2)}, u32[]{:S(2)}) collective-permute-start(bf16[256,768]{1,0:T(8,128)(2,1)S(1)} %pad_maximum_fusion.9), channel_id=1, source_target_pairs={{0,12},{4,8},{8,4},{12,0},{16,28},{20,24},{24,20},{28,16},{1,13},{... | collective-permute-start | bytes 1179656 | tf_op jit(solution)/shard_map/ppermute | solution.py:23
  101.4 71.8 %collective-permute-start.11 = (bf16[2,2,2,2,96,768]{5,4,2,3,0,1:T(8,128)(2,1)}, bf16[2,2,2,2,96,768]{5,4,2,3,0,1:T(8,128)(2,1)}, u32[]{:S(2)}, u32[]{:S(2)}) collective-permute-start(bf16[2,2,2,2,96,768]{5,4,2,3,0,1:T(8,128)(2,1)} %bitcast.303), channel_id=1, source_target_pairs={{0,4},{4,0},{8,12},{12,8},{16,20},{20,16},{24,28},{28,24},{1,5},{5... | collective-permute-start | bytes 7077896 | tf_op jit(solution)/shard_map/ppermute | solution.py:23
  133.8 42.8 %collective-permute-start.9 = (bf16[2,2,2,2,24,3072]{5,4,2,3,1,0:T(8,128)(2,1)}, bf16[2,2,2,2,24,3072]{5,4,2,3,1,0:T(8,128)(2,1)}, u32[]{:S(2)}, u32[]{:S(2)}) collective-permute-start(bf16[2,2,2,2,24,3072]{5,4,2,3,1,0:T(8,128)(2,1)} %bitcast.302), channel_id=1, source_target_pairs={{0,4},{4,0},{8,12},{12,8},{16,20},{20,16},{24,28},{28,24},{1,5},{5... | collective-permute-start | bytes 7077896 | tf_op jit(solution)/shard_map/ppermute | solution.py:23
  143.1 11.9 %collective-permute-start.7 = (bf16[256,768]{1,0:T(8,128)(2,1)S(1)}, bf16[256,768]{1,0:T(8,128)(2,1)S(1)}, u32[]{:S(2)}, u32[]{:S(2)}) collective-permute-start(bf16[256,768]{1,0:T(8,128)(2,1)S(1)} %get-tuple-element.108), channel_id=1, source_target_pairs={{0,8},{4,12},{8,0},{12,4},{16,24},{20,28},{24,16},{28,20},{1,9},{5... | collective-permute-start | bytes 1179656 | tf_op jit(solution)/shard_map/ppermute | solution.py:23
  146.4 15.9 %collective-permute-start.8 = (bf16[256,768]{1,0:T(8,128)(2,1)S(1)}, bf16[256,768]{1,0:T(8,128)(2,1)S(1)}, u32[]{:S(2)}, u32[]{:S(2)}) collective-permute-start(bf16[256,768]{1,0:T(8,128)(2,1)S(1)} %get-tuple-element.107), channel_id=1, source_target_pairs={{0,12},{4,8},{8,4},{12,0},{16,28},{20,24},{24,20},{28,16},{1,13},{... | collective-permute-start | bytes 1179656 | tf_op jit(solution)/shard_map/ppermute | solution.py:23
  170.5 65.0 %collective-permute-start.34 = (bf16[24,768]{1,0:T(8,128)(2,1)S(1)}, bf16[24,768]{1,0:T(8,128)(2,1)S(1)}, u32[]{:S(2)}, u32[]{:S(2)}) collective-permute-start(bf16[24,768]{1,0:T(8,128)(2,1)S(1)} %dynamic-slice_bitcast_fusion.40), channel_id=1, source_target_pairs={{0,2},{1,3},{2,0},{3,1},{4,6},{5,7},{6,4},{7,5},{8,10},{9,11},{10,... | collective-permute-start | bytes 110600 | tf_op jit(solution)/shard_map/ppermute | solution.py:23
  225.0 13.9 %collective-permute-start.21 = (bf16[2,2,2,2,24,1152]{5,4,3,2,1,0:T(8,128)(2,1)}, bf16[2,2,2,2,24,1152]{5,4,3,2,1,0:T(8,128)(2,1)}, u32[]{:S(2)}, u32[]{:S(2)}) collective-permute-start(bf16[2,2,2,2,24,1152]{5,4,3,2,1,0:T(8,128)(2,1)} %dynamic-slice_bitcast_fusion.2), channel_id=1, source_target_pairs={{0,4},{4,0},{8,12},{12,8},{16,20},{20,16},{24,28},{28,24},{1,5},{5... | collective-permute-start | bytes 2654216 | tf_op jit(solution)/shard_map/ppermute | solution.py:23
  236.1 28.8 %collective-permute-start.12 = (bf16[2,2,2,96,768]{4,3,1,2,0:T(8,128)(2,1)S(1)}, bf16[2,2,2,96,768]{4,3,1,2,0:T(8,128)(2,1)S(1)}, u32[]{:S(2)}, u32[]{:S(2)}) collective-permute-start(bf16[2,2,2,96,768]{4,3,1,2,0:T(8,128)(2,1)S(1)} %copy-done.16), channel_id=1, source_target_pairs={{0,8},{4,12},{8,0},{12,4},{16,24},{20,28},{24,16},{28,20},{1,9},{5... | collective-permute-start | bytes 3538952 | tf_op jit(solution)/shard_map/ppermute | solution.py:23
  237.3 30.3 %collective-permute-start.35 = (bf16[2,2,2,24,3072]{4,3,1,2,0:T(8,128)(2,1)S(1)}, bf16[2,2,2,24,3072]{4,3,1,2,0:T(8,128)(2,1)S(1)}, u32[]{:S(2)}, u32[]{:S(2)}) collective-permute-start(bf16[2,2,2,24,3072]{4,3,1,2,0:T(8,128)(2,1)S(1)} %copy-done.15), channel_id=1, source_target_pairs={{0,16},{4,20},{8,24},{12,28},{16,0},{20,4},{24,8},{28,12},{1,17},{... | collective-permute-start | bytes 3538952 | tf_op jit(solution)/shard_map/ppermute | solution.py:23
  241.1 47.7 %collective-permute-start.22 = (bf16[2,2,2,24,1152]{4,3,2,1,0:T(8,128)(2,1)}, bf16[2,2,2,24,1152]{4,3,2,1,0:T(8,128)(2,1)}, u32[]{:S(2)}, u32[]{:S(2)}) collective-permute-start(bf16[2,2,2,24,1152]{4,3,2,1,0:T(8,128)(2,1)} %dynamic-slice_bitcast_fusion.7), channel_id=1, source_target_pairs={{0,8},{4,12},{8,0},{12,4},{16,24},{20,28},{24,16},{28,20},{1,9},{5... | collective-permute-start | bytes 1327112 | tf_op jit(solution)/shard_map/ppermute | solution.py:23
  243.0 48.0 %collective-permute-start.27 = (bf16[2,2,2,24,1152]{4,3,1,2,0:T(8,128)(2,1)}, bf16[2,2,2,24,1152]{4,3,1,2,0:T(8,128)(2,1)}, u32[]{:S(2)}, u32[]{:S(2)}) collective-permute-start(bf16[2,2,2,24,1152]{4,3,1,2,0:T(8,128)(2,1)} %dynamic-slice_bitcast_fusion.6), channel_id=1, source_target_pairs={{0,16},{4,20},{8,24},{12,28},{16,0},{20,4},{24,8},{28,12},{1,17},{... | collective-permute-start | bytes 1327112 | tf_op jit(solution)/shard_map/ppermute | solution.py:23
  266.1 64.3 %collective-permute-start.39 = (bf16[2,2,96,768]{3,2,0,1:T(8,128)(2,1)}, bf16[2,2,96,768]{3,2,0,1:T(8,128)(2,1)}, u32[]{:S(2)}, u32[]{:S(2)}) collective-permute-start(bf16[2,2,96,768]{3,2,0,1:T(8,128)(2,1)} %dynamic-slice_bitcast_fusion.4), channel_id=1, source_target_pairs={{0,16},{4,20},{8,24},{12,28},{16,0},{20,4},{24,8},{28,12},{1,17},{... | collective-permute-start | bytes 1769480 | tf_op jit(solution)/shard_map/ppermute | solution.py:23
  270.1 63.5 %collective-permute-start.36 = (bf16[2,2,24,3072]{3,2,0,1:T(8,128)(2,1)}, bf16[2,2,24,3072]{3,2,0,1:T(8,128)(2,1)}, u32[]{:S(2)}, u32[]{:S(2)}) collective-permute-start(bf16[2,2,24,3072]{3,2,0,1:T(8,128)(2,1)} %dynamic-slice_bitcast_fusion.3), channel_id=1, source_target_pairs={{0,8},{4,12},{8,0},{12,4},{16,24},{20,28},{24,16},{28,20},{1,9},{5... | collective-permute-start | bytes 1769480 | tf_op jit(solution)/shard_map/ppermute | solution.py:23
  287.2 37.7 %collective-permute-start.16 = (bf16[2,2,2,2,24,640]{5,4,3,2,1,0:T(8,128)(2,1)S(1)}, bf16[2,2,2,2,24,640]{5,4,3,2,1,0:T(8,128)(2,1)S(1)}, u32[]{:S(2)}, u32[]{:S(2)}) collective-permute-start(bf16[2,2,2,2,24,640]{5,4,3,2,1,0:T(8,128)(2,1)S(1)} %dynamic-slice_bitcast_fusion.5), channel_id=1, source_target_pairs={{0,4},{4,0},{8,12},{12,8},{16,20},{20,16},{24,28},{28,24},{1,5},{5... | collective-permute-start | bytes 1474568 | tf_op jit(solution)/shard_map/ppermute | solution.py:23
  288.8 16.1 %collective-permute-start.13 = (bf16[256,768]{1,0:T(8,128)(2,1)S(1)}, bf16[256,768]{1,0:T(8,128)(2,1)S(1)}, u32[]{:S(2)}, u32[]{:S(2)}) collective-permute-start(bf16[256,768]{1,0:T(8,128)(2,1)S(1)} %get-tuple-element.106), channel_id=1, source_target_pairs={{0,4},{4,0},{8,12},{12,8},{16,20},{20,16},{24,28},{28,24},{1,5},{5... | collective-permute-start | bytes 1179656 | tf_op jit(solution)/shard_map/ppermute | solution.py:23
  303.9 12.1 %collective-permute-start.14 = (bf16[256,768]{1,0:T(8,128)(2,1)S(1)}, bf16[256,768]{1,0:T(8,128)(2,1)S(1)}, u32[]{:S(2)}, u32[]{:S(2)}) collective-permute-start(bf16[256,768]{1,0:T(8,128)(2,1)S(1)} %get-tuple-element.105), channel_id=1, source_target_pairs={{0,8},{4,12},{8,0},{12,4},{16,24},{20,28},{24,16},{28,20},{1,9},{5... | collective-permute-start | bytes 1179656 | tf_op jit(solution)/shard_map/ppermute | solution.py:23
  304.9 14.3 %collective-permute-start.15 = (bf16[256,768]{1,0:T(8,128)(2,1)S(1)}, bf16[256,768]{1,0:T(8,128)(2,1)S(1)}, u32[]{:S(2)}, u32[]{:S(2)}) collective-permute-start(bf16[256,768]{1,0:T(8,128)(2,1)S(1)} %get-tuple-element.104), channel_id=1, source_target_pairs={{0,12},{4,8},{8,4},{12,0},{16,28},{20,24},{24,20},{28,16},{1,13},{... | collective-permute-start | bytes 1179656 | tf_op jit(solution)/shard_map/ppermute | solution.py:23
  336.5 14.5 %collective-permute-start.37 = (bf16[2,24,3072]{2,1,0:T(8,128)(2,1)S(1)}, bf16[2,24,3072]{2,1,0:T(8,128)(2,1)S(1)}, u32[]{:S(2)}, u32[]{:S(2)}) collective-permute-start(bf16[2,24,3072]{2,1,0:T(8,128)(2,1)S(1)} %dynamic-slice_bitcast_fusion.9), channel_id=1, source_target_pairs={{0,1},{1,0},{2,3},{3,2},{4,5},{5,4},{6,7},{7,6},{8,9},{9,8},{10,11... | collective-permute-start | bytes 884744 | tf_op jit(solution)/shard_map/ppermute | solution.py:23
  341.8 17.6 %collective-permute-start.41 = (bf16[96,768]{1,0:T(8,128)(2,1)S(1)}, bf16[96,768]{1,0:T(8,128)(2,1)S(1)}, u32[]{:S(2)}, u32[]{:S(2)}) collective-permute-start(bf16[96,768]{1,0:T(8,128)(2,1)S(1)} %dynamic-slice_bitcast_fusion.30), channel_id=1, source_target_pairs={{0,2},{1,3},{2,0},{3,1},{4,6},{5,7},{6,4},{7,5},{8,10},{9,11},{10,... | collective-permute-start | bytes 442376 | tf_op jit(solution)/shard_map/ppermute | solution.py:23
  (51 other events, 303.7 us)
